TPU v7x, 32 devices: a whole 2x2x4 slice. The times are simulated.
32 devices in a mesh: cent: 8 (over y, x, core), rep: 4 (over z).
Axes of the slice: x: 2, y: 2, z: 4, core: 2. Of those that a mesh axis runs over, the one named last changes fastest.
Arguments:
- points: bfloat16 [16384, 1024], P(('cent', 'rep')), may hold values from -6 to 6
- centroids: bfloat16 [4096, 1024], P('cent'), may hold values from -6 to 6
- owners: int32 [16384, 2], P(('cent', 'rep')), may hold values from 0 to 7, all different within a row; in each aligned block of 512 rows (0 to 511, 512 to 1023, ...) at most 320 rows name the same one
- blocks: int32 [16384, 2, 4], P(('cent', 'rep')), may hold values from 0 to 7, all different within a row
- duals: float32 [4096], P('cent'), may hold values from -1 to 1
Outputs:
- new_centroids: bfloat16 [4096, 1024], P('cent')
- duals_out: float32 [4096], P('cent')
Inputs may be any that keep to these rules, and one draw needn't show every extreme that they name: `owners`: each point names 2 different owner shards; among the points of one device no shard is named more than 320 times, a bound that some block reaches. `blocks`: the 4 block numbers that a point names within one owner shard differ.
All inputs are finite; a program needn't handle non-finite values.
Results may differ from a plain program's by a relative error of at most 0.012.
The roundings to bfloat16 on the way count: a program that leaves them out, or rounds other values in their place, can miss the bound.
Values may be sent and summed in bfloat16 or wider, within the bound.
A program may use at most 64 MiB of HBM per device.

v0:
```python
import jax
import jax.numpy as jnp
from jax import lax
from jax.sharding import PartitionSpec as P

BLOCKS_DEV = 8
CAND = 4
SINK = 3
ITERS = 2


softness_factor = 0.02
EPSILON = 1e-06


def normalize(values):
    widened = values.astype(jnp.float32)
    return (
        widened * lax.rsqrt(jnp.mean(widened * widened, axis=-1, keepdims=True) + EPSILON)
    ).astype(jnp.bfloat16)


def candidate_mask(labels_in, block_span):
    member = jnp.any(
        labels_in[:, :, None] == jnp.arange(BLOCKS_DEV, dtype=jnp.int32)[None, None, :], axis=1
    )
    return jnp.repeat(member.astype(jnp.float32), block_span, axis=1)


def kernel_of(slot_rows, slot_mask, centroid_unit, feature_dimension):
    affinity_scores = lax.dot_general(
        slot_rows, centroid_unit, (((1,), (1,)), ((), ())), preferred_element_type=jnp.float32
    ) / (feature_dimension * softness_factor)
    return jnp.exp(affinity_scores) * slot_mask


def body(points, centroids, owners, blocks, duals):
    point_rows, feature_dimension = points.shape
    shard_rows = centroids.shape[0]
    shards = lax.axis_size("cent")
    replicas = lax.axis_size("rep")
    routes = owners.shape[1]
    capacity = 5 * point_rows // shards
    block_span = shard_rows // BLOCKS_DEV
    target = point_rows * replicas / shard_rows
    unit_rows = normalize(points)
    flat_owner = owners.reshape(-1)
    flat_point = jnp.arange(point_rows * routes, dtype=jnp.int32) // routes
    onehot = (flat_owner[:, None] == jnp.arange(shards, dtype=jnp.int32)[None, :]).astype(jnp.int32)
    position = jnp.sum((jnp.cumsum(onehot, axis=0) - onehot) * onehot, axis=1)
    outgoing = (
        jnp.zeros((shards, capacity, feature_dimension), jnp.bfloat16)
        .at[flat_owner, position]
        .set(unit_rows[flat_point])
    )
    labels = (
        jnp.full((shards, capacity, CAND), -1, jnp.int32)
        .at[flat_owner, position]
        .set(blocks.reshape(-1, CAND))
    )
    first_unit = normalize(centroids)
    received_rows = (
        lax.all_to_all(outgoing, "cent", split_axis=0, concat_axis=0, tiled=True),
        lax.all_to_all(labels, "cent", split_axis=0, concat_axis=0, tiled=True),
    )
    slot_rows = received_rows[0].reshape(-1, feature_dimension)
    slot_mask = candidate_mask(received_rows[1].reshape(-1, CAND), block_span)
    first_kernel = kernel_of(slot_rows, slot_mask, first_unit, feature_dimension)
    current = centroids
    duals_now = duals
    for loop_counter in range(ITERS):
        if loop_counter == 0:
            kernel = first_kernel
        else:
            kernel = kernel_of(slot_rows, slot_mask, normalize(current), feature_dimension)
        for turn_index in range(SINK + 1):
            scaling = jnp.exp(duals_now)
            partial_rows = jnp.dot(kernel, scaling, precision=lax.Precision.HIGHEST).reshape(
                shards, capacity
            )
            returned = lax.all_to_all(partial_rows, "cent", split_axis=0, concat_axis=0, tiled=True)
            totals = jnp.sum(returned[flat_owner, position].reshape(point_rows, routes), axis=1)
            inverse = 1.0 / totals
            spread = (
                jnp.zeros((shards, capacity), jnp.float32)
                .at[flat_owner, position]
                .set(inverse[flat_point])
            )
            row_scale = lax.all_to_all(
                spread, "cent", split_axis=0, concat_axis=0, tiled=True
            ).reshape(-1)
            if turn_index < SINK:
                local_mass = jnp.dot(row_scale, kernel, precision=lax.Precision.HIGHEST) * scaling
                column_mass = lax.psum(local_mass, "rep")
                duals_now = duals_now + jnp.log(2.0 * target) - jnp.log(column_mass + target)
        weights = (row_scale[:, None] * kernel * scaling[None, :]).astype(jnp.bfloat16)
        share_sums = lax.psum_scatter(
            lax.dot_general(
                weights, slot_rows, (((0,), (0,)), ((), ())), preferred_element_type=jnp.float32
            ),
            "rep",
            scatter_dimension=0,
            tiled=True,
        )
        current = lax.all_gather(normalize(share_sums), "rep", axis=0, tiled=True)
    return (current, duals_now)


def solution(mesh):
    return jax.shard_map(
        body,
        mesh=mesh,
        in_specs=(
            P(("cent", "rep"), None),
            P("cent", None),
            P(("cent", "rep"), None),
            P(("cent", "rep"), None, None),
            P("cent"),
        ),
        out_specs=(P("cent", None), P("cent")),
        check_vma=False,
    )
```

profile of v0, /device:TPU:0, one launch (start us, length us, event | category | flops | bytes accessed | tf_op | source)
XLA Modules:
  0.0 701.2 jit_solution(5911123965353449566)
XLA Ops:
  18.5 5.2 all-to-all-start.1
  24.2 16.4 %scatter_custom_fusion = bf16[2560,1024]{1,0:T(8,128)(2,1)} fusion(s32[1024]{0:T(1024)S(1)} %get-tuple-element.12, bf16[]{:T(256)} %constant.47.clone.1, bf16[512,1024]{1,0:T(8,128)(2,1)S(1)} %fusion.9, s32[1024]{0:T(1024)S(1)} %get-tuple-element.11), kind=kCustom, calls=%fused_computation.39 | custom fusion | bytes 5242882
  40.7 4.8 all-to-all-start
  48.9 6.0 copy.45
  54.8 51.0 %all-to-all-done = bf16[8,320,1024]{2,1,0:T(8,128)(2,1)} async-done(((bf16[8,320,1024]{2,1,0:T(8,128)(2,1)}), bf16[8,320,1024]{2,1,0:T(8,128)(2,1)}, u32[]{:S(2)}, u32[]{:S(2)}) %all-to-all-start) | async-done | bytes 5242912 | tf_op jit(solution)/shard_map/all_to_all | solution.py:63
  105.8 8.9 %exponential_multiply_fusion.1 = f32[2560,512]{1,0:T(8,128)S(1)} fusion(f32[2560,512]{1,0:T(8,128)} %copy.45, bf16[2560,1024]{1,0:T(8,128)(2,1)} %bitcast.4, bf16[512,1024]{1,0:T(8,128)(2,1)S(1)} %copy-done.3, f32[512]{0:T(512)S(1)} %add_rsqrt_fusion.1), kind=kOutput, calls=%fused_computation.30 | convolution fusion | flops 2688548864 | bytes 16779264 | tf_op jit(solution)/shard_map/dot_general | solution.py:31
  121.7 7.1 %all_to_all.178 = f32[8,1,320]{2,1,0:T(1,128)S(1)} all-to-all(f32[8,1,320]{2,1,0:T(1,128)S(1)} %all_to_all.120), channel_id=1, replica_groups=mesh['cent'=8,'rep'=4] {'cent'}, dimensions={0} | all-to-all | bytes 20480 | tf_op jit(solution)/shard_map/all_to_all | solution.py:81
  128.8 6.7 gather_fusion
  135.9 6.9 gather_fusion.1
  147.2 7.2 %all_to_all.179 = f32[8,1,320]{2,1,0:T(1,128)S(1)} all-to-all(f32[8,1,320]{2,1,0:T(1,128)S(1)} %all_to_all.123), channel_id=1, replica_groups=mesh['cent'=8,'rep'=4] {'cent'}, dimensions={0} | all-to-all | bytes 20480 | tf_op jit(solution)/shard_map/all_to_all | solution.py:89
  154.5 5.1 fusion.48
  159.6 12.0 %psum.42 = f32[512]{0:T(512)S(1)} all-reduce(f32[512]{0:T(512)S(1)} %exponential_multiply_fusion.4), channel_id=1, replica_groups=mesh['cent'=8,'rep'=4] {'rep'}, use_global_device_ids=true, to_apply=%region_10.11 | all-reduce | flops 512 | bytes 4096 | tf_op jit(solution)/shard_map/psum | solution.py:94
  171.6 6.9 convolution_reduce_fusion.6
  178.6 7.1 %all_to_all.180 = f32[8,1,320]{2,1,0:T(1,128)S(1)} all-to-all(f32[8,1,320]{2,1,0:T(1,128)S(1)} %all_to_all.125), channel_id=1, replica_groups=mesh['cent'=8,'rep'=4] {'cent'}, dimensions={0} | all-to-all | bytes 20480 | tf_op jit(solution)/shard_map/all_to_all | solution.py:81
  185.7 6.7 gather_fusion.2
  192.8 6.9 gather_fusion.3
  204.1 7.1 %all_to_all.181 = f32[8,1,320]{2,1,0:T(1,128)S(1)} all-to-all(f32[8,1,320]{2,1,0:T(1,128)S(1)} %all_to_all.128), channel_id=1, replica_groups=mesh['cent'=8,'rep'=4] {'cent'}, dimensions={0} | all-to-all | bytes 20480 | tf_op jit(solution)/shard_map/all_to_all | solution.py:89
  211.3 5.1 fusion.49
  216.3 8.6 %psum.43 = f32[512]{0:T(512)S(1)} all-reduce(f32[512]{0:T(512)S(1)} %mul.127), channel_id=1, replica_groups=mesh['cent'=8,'rep'=4] {'rep'}, use_global_device_ids=true, to_apply=%region_13.14 | all-reduce | flops 512 | bytes 4096 | tf_op jit(solution)/shard_map/psum | solution.py:94
  224.9 6.9 convolution_reduce_fusion.5
  231.9 7.1 %all_to_all.182 = f32[8,1,320]{2,1,0:T(1,128)S(1)} all-to-all(f32[8,1,320]{2,1,0:T(1,128)S(1)} %all_to_all.130), channel_id=1, replica_groups=mesh['cent'=8,'rep'=4] {'cent'}, dimensions={0} | all-to-all | bytes 20480 | tf_op jit(solution)/shard_map/all_to_all | solution.py:81
  239.0 6.7 gather_fusion.4
  246.1 6.9 gather_fusion.5
  257.4 7.1 %all_to_all.183 = f32[8,1,320]{2,1,0:T(1,128)S(1)} all-to-all(f32[8,1,320]{2,1,0:T(1,128)S(1)} %all_to_all.133), channel_id=1, replica_groups=mesh['cent'=8,'rep'=4] {'cent'}, dimensions={0} | all-to-all | bytes 20480 | tf_op jit(solution)/shard_map/all_to_all | solution.py:89
  264.6 5.1 fusion.50
  269.6 10.4 %psum.44 = f32[512]{0:T(512)S(1)} all-reduce(f32[512]{0:T(512)S(1)} %exponential_multiply_fusion.3), channel_id=1, replica_groups=mesh['cent'=8,'rep'=4] {'rep'}, use_global_device_ids=true, to_apply=%region_16.17 | all-reduce | flops 512 | bytes 4096 | tf_op jit(solution)/shard_map/psum | solution.py:94
  280.0 6.9 convolution_reduce_fusion.4
  287.1 7.5 %all_to_all.184 = f32[8,1,320]{2,1,0:T(1,128)S(1)} all-to-all(f32[8,1,320]{2,1,0:T(1,128)S(1)} %all_to_all.135), channel_id=1, replica_groups=mesh['cent'=8,'rep'=4] {'cent'}, dimensions={0} | all-to-all | bytes 20480 | tf_op jit(solution)/shard_map/all_to_all | solution.py:81
  294.5 6.7 gather_fusion.6
  301.6 6.9 gather_fusion.7
  312.9 7.1 %all_to_all.185 = f32[8,1,320]{2,1,0:T(1,128)S(1)} all-to-all(f32[8,1,320]{2,1,0:T(1,128)S(1)} %all_to_all.138), channel_id=1, replica_groups=mesh['cent'=8,'rep'=4] {'cent'}, dimensions={0} | all-to-all | bytes 20480 | tf_op jit(solution)/shard_map/all_to_all | solution.py:89
  320.1 8.4 %fusion = f32[512,1024]{1,0:T(8,128)} fusion(bf16[2560,1024]{1,0:T(8,128)(2,1)} %bitcast.4, f32[2560,512]{1,0:T(8,128)} %copy-done.1, f32[512]{0:T(512)S(1)} %fusion.43, f32[2560]{0:T(1024)S(1)} %mul.129), kind=kOutput, calls=%fused_computation.37 | convolution fusion | flops 2688286720 | bytes 12595200 | tf_op jit(solution)/shard_map/dot_general | solution.py:98
  328.5 40.0 %reduce-scatter.3.cloned.1.call-done = f32[128,1024]{1,0:T(8,128)} async-done(((f32[512,1024]{1,0:T(8,128)}), f32[128,1024]{1,0:T(8,128)}) %reduce-scatter.3.cloned.1.call-update) | async-done | bytes 524304 | tf_op jit(solution)/shard_map/reduce_scatter | solution.py:97
  371.7 27.3 %all-gather.3.cloned.1.call-done = bf16[512,1024]{1,0:T(8,128)(2,1)} async-done(((bf16[128,1024]{1,0:T(8,128)(2,1)}), bf16[512,1024]{1,0:T(8,128)(2,1)}) %all-gather.3.cloned.1.call-update) | async-done | bytes 1048592 | tf_op jit(solution)/shard_map/all_gather | solution.py:105
  400.5 7.6 %exponential_multiply_fusion = f32[2560,512]{1,0:T(8,128)S(1)} fusion(f32[2560,512]{1,0:T(8,128)} %copy.45, bf16[2560,1024]{1,0:T(8,128)(2,1)} %bitcast.4, bf16[512,1024]{1,0:T(8,128)(2,1)} %all-gather.3.cloned.1.call-done, f32[512]{0:T(512)S(1)} %add_rsqrt_fusion), kind=kOutput, calls=%fused_computation.28 | convolution fusion | flops 2688548864 | bytes 16779264 | tf_op jit(solution)/shard_map/dot_general | solution.py:31
  410.5 4.5 convolution_reduce_fusion.3
  415.1 8.3 %all_to_all.186 = f32[8,1,320]{2,1,0:T(1,128)S(1)} all-to-all(f32[8,1,320]{2,1,0:T(1,128)S(1)} %all_to_all.140), channel_id=1, replica_groups=mesh['cent'=8,'rep'=4] {'cent'}, dimensions={0} | all-to-all | bytes 20480 | tf_op jit(solution)/shard_map/all_to_all | solution.py:81
  423.4 6.7 gather_fusion.8
  430.5 6.9 gather_fusion.9
  441.8 7.1 %all_to_all.187 = f32[8,1,320]{2,1,0:T(1,128)S(1)} all-to-all(f32[8,1,320]{2,1,0:T(1,128)S(1)} %all_to_all.143), channel_id=1, replica_groups=mesh['cent'=8,'rep'=4] {'cent'}, dimensions={0} | all-to-all | bytes 20480 | tf_op jit(solution)/shard_map/all_to_all | solution.py:89
  449.0 5.1 fusion.51
  454.0 10.2 %psum.45 = f32[512]{0:T(512)S(1)} all-reduce(f32[512]{0:T(512)S(1)} %mul.141), channel_id=1, replica_groups=mesh['cent'=8,'rep'=4] {'rep'}, use_global_device_ids=true, to_apply=%region_24.25 | all-reduce | flops 512 | bytes 4096 | tf_op jit(solution)/shard_map/psum | solution.py:94
  464.2 6.9 convolution_reduce_fusion.2
  471.2 7.1 %all_to_all.188 = f32[8,1,320]{2,1,0:T(1,128)S(1)} all-to-all(f32[8,1,320]{2,1,0:T(1,128)S(1)} %all_to_all.145), channel_id=1, replica_groups=mesh['cent'=8,'rep'=4] {'cent'}, dimensions={0} | all-to-all | bytes 20480 | tf_op jit(solution)/shard_map/all_to_all | solution.py:81
  478.3 6.7 gather_fusion.10
  485.4 6.9 gather_fusion.11
  496.7 7.3 %all_to_all.189 = f32[8,1,320]{2,1,0:T(1,128)S(1)} all-to-all(f32[8,1,320]{2,1,0:T(1,128)S(1)} %all_to_all.148), channel_id=1, replica_groups=mesh['cent'=8,'rep'=4] {'cent'}, dimensions={0} | all-to-all | bytes 20480 | tf_op jit(solution)/shard_map/all_to_all | solution.py:89
  504.1 5.1 fusion.52
  509.1 8.6 %psum.46 = f32[512]{0:T(512)S(1)} all-reduce(f32[512]{0:T(512)S(1)} %exponential_multiply_fusion.2), channel_id=1, replica_groups=mesh['cent'=8,'rep'=4] {'rep'}, use_global_device_ids=true, to_apply=%region_27.28 | all-reduce | flops 512 | bytes 4096 | tf_op jit(solution)/shard_map/psum | solution.py:94
  517.7 6.9 convolution_reduce_fusion.1
  524.8 7.1 %all_to_all.190 = f32[8,1,320]{2,1,0:T(1,128)S(1)} all-to-all(f32[8,1,320]{2,1,0:T(1,128)S(1)} %all_to_all.150), channel_id=1, replica_groups=mesh['cent'=8,'rep'=4] {'cent'}, dimensions={0} | all-to-all | bytes 20480 | tf_op jit(solution)/shard_map/all_to_all | solution.py:81
  531.8 6.7 gather_fusion.12
  538.9 6.9 gather_fusion.13
  550.2 7.1 %all_to_all.191 = f32[8,1,320]{2,1,0:T(1,128)S(1)} all-to-all(f32[8,1,320]{2,1,0:T(1,128)S(1)} %all_to_all.153), channel_id=1, replica_groups=mesh['cent'=8,'rep'=4] {'cent'}, dimensions={0} | all-to-all | bytes 20480 | tf_op jit(solution)/shard_map/all_to_all | solution.py:89
  557.4 5.1 fusion.53
  562.5 10.4 %psum.47 = f32[512]{0:T(512)S(1)} all-reduce(f32[512]{0:T(512)S(1)} %mul.143), channel_id=1, replica_groups=mesh['cent'=8,'rep'=4] {'rep'}, use_global_device_ids=true, to_apply=%region_30.31 | all-reduce | flops 512 | bytes 4096 | tf_op jit(solution)/shard_map/psum | solution.py:94
  573.5 6.9 convolution_reduce_fusion
  580.5 7.1 %all_to_all.192 = f32[8,1,320]{2,1,0:T(1,128)S(1)} all-to-all(f32[8,1,320]{2,1,0:T(1,128)S(1)} %all_to_all.155), channel_id=1, replica_groups=mesh['cent'=8,'rep'=4] {'cent'}, dimensions={0} | all-to-all | bytes 20480 | tf_op jit(solution)/shard_map/all_to_all | solution.py:81
  587.6 6.7 gather_fusion.14
  594.6 6.9 gather_fusion.15
  605.9 7.1 %all_to_all.193 = f32[8,1,320]{2,1,0:T(1,128)S(1)} all-to-all(f32[8,1,320]{2,1,0:T(1,128)S(1)} %all_to_all.158), channel_id=1, replica_groups=mesh['cent'=8,'rep'=4] {'cent'}, dimensions={0} | all-to-all | bytes 20480 | tf_op jit(solution)/shard_map/all_to_all | solution.py:89
  613.1 8.3 %fusion.1 = f32[512,1024]{1,0:T(8,128)} fusion(bf16[2560,1024]{1,0:T(8,128)(2,1)} %bitcast.4, f32[2560,512]{1,0:T(8,128)} %copy-done, f32[512]{0:T(512)S(1)} %get-tuple-element.2, f32[2560]{0:T(1024)S(1)} %mul.144), kind=kOutput, calls=%fused_computation.38 | convolution fusion | flops 2688286720 | bytes 12595200 | tf_op jit(solution)/shard_map/dot_general | solution.py:98
  621.5 40.0 %reduce-scatter.5.cloned.1.call-done = f32[128,1024]{1,0:T(8,128)} async-done(((f32[512,1024]{1,0:T(8,128)}), f32[128,1024]{1,0:T(8,128)}) %reduce-scatter.5.cloned.1.call-update) | async-done | bytes 524304 | tf_op jit(solution)/shard_map/reduce_scatter | solution.py:97
  664.6 27.4 %all-gather.5.cloned.1.call-done = bf16[512,1024]{1,0:T(8,128)(2,1)} async-done(((bf16[128,1024]{1,0:T(8,128)(2,1)}), bf16[512,1024]{1,0:T(8,128)(2,1)}) %all-gather.5.cloned.1.call-update) | async-done | bytes 1048592 | tf_op jit(solution)/shard_map/all_gather | solution.py:105
  (142 shorter events, 74.7 us)
Async XLA Ops:
  7.2 16.5 %copy-start.2 = (bf16[512,1024]{1,0:T(8,128)(2,1)S(1)}, bf16[512,1024]{1,0:T(8,128)(2,1)}, u32[]{:S(2)}) copy-start(bf16[512,1024]{1,0:T(8,128)(2,1)} %param.5) | copy-start | bytes 3145732
  18.5 22.1 %all-to-all-start.1 = ((s32[8,320,4]{1,2,0:T(4,128)}), s32[8,320,4]{1,2,0:T(4,128)S(1)}, u32[]{:S(2)}, u32[]{:S(2)}) async-start(s32[8,320,4]{1,2,0:T(4,128)} %copy.43), calls=%async_computation.1 | async-start | bytes 98304 | tf_op jit(solution)/shard_map/all_to_all | solution.py:64
  40.7 4.9 copy-start.4
  40.7 4.9 copy-start.3
  40.7 65.1 %all-to-all-start = ((bf16[8,320,1024]{2,1,0:T(8,128)(2,1)}), bf16[8,320,1024]{2,1,0:T(8,128)(2,1)}, u32[]{:S(2)}, u32[]{:S(2)}) async-start(bf16[8,320,1024]{2,1,0:T(8,128)(2,1)} %bitcast.125), calls=%async_computation | async-start | bytes 10485760 | tf_op jit(solution)/shard_map/all_to_all | solution.py:63
  45.5 323.1 %reduce-scatter.3.cloned.1.call-start = ((), (), s32[]{:S(2)}) async-start(), calls=%async_computation.20 | async-start | bytes 2621440 | tf_op jit(solution)/shard_map/reduce_scatter | solution.py:97
  114.7 2.4 copy-start.1
  328.5 70.5 %all-gather.3.cloned.1.call-start = ((), (), s32[]{:S(2)}) async-start(), calls=%async_computation.21 | async-start | bytes 1310720 | tf_op jit(solution)/shard_map/all_gather | solution.py:105
  371.6 290.0 %reduce-scatter.5.cloned.1.call-start = ((), (), s32[]{:S(2)}) async-start(), calls=%async_computation.22 | async-start | bytes 2621440 | tf_op jit(solution)/shard_map/reduce_scatter | solution.py:97
  408.1 2.3 copy-start
  621.5 70.5 %all-gather.5.cloned.1.call-start = ((), (), s32[]{:S(2)}) async-start(), calls=%async_computation.23 | async-start | bytes 1310720 | tf_op jit(solution)/shard_map/all_gather | solution.py:105
Sparse Core Ops, SparseCore 0:
  328.6 39.9 reduce-scatter.2
  371.7 27.1 all-gather.2
  621.6 39.9 reduce-scatter.4
  664.7 27.1 all-gather.4
where the time goes:
time: 711 us; the launch traced here: 701 us
  local copies, waits for them, and re-layouts  186 us (26%)
  waiting for transfers between devices  186 us (26%)
  blocking collectives  175 us (25%)
  matrix products  114 us (16%)
  between operations  14.9 us (2%)
  other arithmetic  14.6 us (2%)
  starting transfers between devices  10.2 us (1%)
    reduce_scatter x2, waiting for transfers between devices, body(): lax.psum_scatter(lax.dot_general(weights, slot_rows, (((0,), (0,)), ((),...  80.1 us
    unnamed x31, local copies, waits for them, and re-layouts  63.3 us
    psum x6, blocking collectives, body(): column_mass = lax.psum(local_mass, 'rep')  60 us
    all_to_all x8, blocking collectives, body(): lax.all_to_all(partial_rows, 'cent', split_axis=0, concat_axis=0, tiled=T...  58.3 us
    all_to_all x8, blocking collectives, body(): lax.all_to_all(spread, 'cent', split_axis=0, concat_axis=0, tiled=True)  57 us
    gather x8, local copies, waits for them, and re-layouts, body(): inverse[flat_point]  54.9 us
    all_gather x2, waiting for transfers between devices, body(): current = lax.all_gather(normalize(share_sums), 'rep', axis=0, tiled=True)  54.7 us
    gather x8, local copies, waits for them, and re-layouts, body(): returned[flat_owner, position].reshape(point_rows, routes)  53.7 us
  transfers between devices with their start and end apart: 6, of which 5 were waited for; matrix products, arithmetic and copies ran while one was open for 4% of the time, Pallas kernels for 0%

commit v1 on v0

--- a/solution.py
+++ b/solution.py
@@ -1,12 +1,20 @@
+import functools
+
 import jax
 import jax.numpy as jnp
 from jax import lax
+from jax.experimental import pallas as pl
+from jax.experimental.pallas import tpu as pltpu
 from jax.sharding import PartitionSpec as P
 
 BLOCKS_DEV = 8
 CAND = 4
 SINK = 3
 ITERS = 2
+LANES = 128
+SUBLANES = 8
+MESH = pl.DeviceIdType.MESH
+VMEM_LIMIT = 64000000
 
 
 softness_factor = 0.02
@@ -34,7 +42,7 @@
     return jnp.exp(affinity_scores) * slot_mask
 
 
-def body(points, centroids, owners, blocks, duals):
+def routed_body(points, centroids, owners, blocks, duals):
     point_rows, feature_dimension = points.shape
     shard_rows = centroids.shape[0]
     shards = lax.axis_size("cent")
@@ -106,7 +114,413 @@
     return (current, duals_now)
 
 
+def fused_kernel(
+    dims,
+    points_ref,
+    centroids_ref,
+    mask_ref,
+    duals_ref,
+    out_ref,
+    duals_out_ref,
+    units,
+    masks,
+    kern,
+    cunit,
+    scale_cols,
+    mass_cols,
+    sums,
+    row_parts,
+    col_parts,
+    sums_out,
+    sums_in,
+    unit_send,
+    unit_recv,
+    mask_send,
+    mask_recv,
+    row_send,
+    row_recv,
+    col_send,
+    col_recv,
+    sum_send,
+    sum_recv,
+    new_send,
+    new_recv,
+):
+    shards, replicas, point_rows, shard_rows, features = dims
+    span = shard_rows // BLOCKS_DEV
+    pieces = 4
+    piece = point_rows // pieces
+    dual_rows = shard_rows // LANES
+    share = shard_rows // replicas
+    target = point_rows * replicas / shard_rows
+    inverse_soft = 1.0 / (features * softness_factor)
+
+    me = lax.axis_index("cent")
+    z = lax.axis_index("rep")
+    core = me % 2
+    xpos = (me // 2) % 2
+    ypos = me // 4
+
+    def rel(direction):
+        dc, dx, dy = direction % 2, (direction // 2) % 2, direction // 4
+        c = 1 - core if dc else core
+        x = 1 - xpos if dx else xpos
+        y = 1 - ypos if dy else ypos
+        return (y * 2 + x) * 2 + c
+
+    peer = [rel(d) for d in range(shards)]
+    zpeer = [(z + k) % replicas for k in range(replicas)]
+
+    barrier = pltpu.get_barrier_semaphore()
+    for d in range(1, shards):
+        pl.semaphore_signal(barrier, inc=1, device_id=(peer[d], z), device_id_type=MESH)
+    for k in range(1, replicas):
+        pl.semaphore_signal(barrier, inc=1, device_id=(me, zpeer[k]), device_id_type=MESH)
+    pl.semaphore_wait(barrier, shards - 1 + replicas - 1)
+
+    mask_copies = []
+    for d in range(1, shards):
+        copy = pltpu.make_async_remote_copy(
+            src_ref=mask_ref.at[peer[d]],
+            dst_ref=masks.at[d],
+            send_sem=mask_send.at[d],
+            recv_sem=mask_recv.at[d],
+            device_id=(peer[d], z),
+            device_id_type=MESH,
+        )
+        copy.start()
+        mask_copies.append(copy)
+    masks[0] = mask_ref[me]
+
+    unit_copies = {}
+
+    def push(slot, chunk, direction):
+        rows = pl.ds(chunk * piece, piece)
+        copy = pltpu.make_async_remote_copy(
+            src_ref=units.at[slot, rows],
+            dst_ref=units.at[slot ^ direction, rows],
+            send_sem=unit_send.at[slot, chunk, direction // 2],
+            recv_sem=unit_recv.at[slot ^ direction, chunk],
+            device_id=(peer[direction], z),
+            device_id_type=MESH,
+        )
+        copy.start()
+        unit_copies[(slot, chunk, direction)] = copy
+
+    def arrive(slot, chunk):
+        rows = pl.ds(chunk * piece, piece)
+        pltpu.make_async_copy(
+            units.at[slot, rows], units.at[slot, rows], unit_recv.at[slot, chunk]
+        ).wait()
+
+    order_x = (0, 1, 2, 3)
+    order_y = (2, 3, 0, 1)
+    for step in (0, 2, 1, 3):
+        rows = pl.ds(step * piece, piece)
+        units[0, rows] = normalize(points_ref[rows])
+        if step == 0:
+            push(0, 0, 2)
+        if step == 2:
+            push(0, 2, 4)
+        if step == 1:
+            push(0, 1, 2)
+            push(0, 2, 2)
+        if step == 3:
+            push(0, 3, 4)
+            push(0, 3, 2)
+            push(0, 0, 4)
+            push(0, 1, 4)
+    for step in range(pieces):
+        push(0, step, 1)
+
+    cunit[...] = normalize(centroids_ref[...])
+
+    def block_kernel(slot):
+        scores = lax.dot_general(
+            cunit[...],
+            units[slot],
+            (((1,), (1,)), ((), ())),
+            preferred_element_type=jnp.float32,
+        )
+        marks = masks[slot]
+        for b in range(BLOCKS_DEV):
+            rows = slice(b * span, (b + 1) * span)
+            kern[slot, rows, :] = jnp.exp(scores[rows] * inverse_soft) * marks[b : b + 1, :]
+
+    block_kernel(0)
+    for step in range(pieces):
+        tx, ty = order_x[step], order_y[step]
+        arrive(2, tx)
+        if step < 2:
+            push(2, tx, 4)
+        push(2, tx, 1)
+        arrive(4, ty)
+        if step < 2:
+            push(4, ty, 2)
+        push(4, ty, 1)
+        if step == 1:
+            for copy in mask_copies:
+                copy.wait()
+            for chunk in range(pieces):
+                arrive(1, chunk)
+            block_kernel(1)
+        if step >= 2:
+            arrive(6, order_x[step - 2])
+            push(6, order_x[step - 2], 1)
+            arrive(6, order_y[step - 2])
+            push(6, order_y[step - 2], 1)
+    for slot in (2, 4, 6, 3, 5, 7):
+        if slot % 2:
+            for chunk in range(pieces):
+                arrive(slot, chunk)
+        block_kernel(slot)
+    for copy in unit_copies.values():
+        copy.wait_send()
+
+    duals_now = duals_ref[...]
+    groups = shard_rows // SUBLANES
+    tiles = point_rows // LANES
+
+    def spread_scale(scaling):
+        for t in range(dual_rows):
+            row = jnp.broadcast_to(scaling[t : t + 1, :], (LANES, LANES))
+            scale_cols[pl.ds(t * LANES, LANES), :] = row.T
+
+    def row_pass():
+        def step(g, acc):
+            rows = pl.ds(pl.multiple_of(g * SUBLANES, SUBLANES), SUBLANES)
+            wide = jnp.concatenate([scale_cols[rows, :]] * tiles, axis=1)
+            return tuple(acc[p] + kern[p, rows, :] * wide for p in range(shards))
+
+        zero = jnp.zeros((SUBLANES, point_rows), jnp.float32)
+        acc = lax.fori_loop(0, groups, step, (zero,) * shards, unroll=2)
+        return jnp.concatenate([jnp.sum(a, axis=0, keepdims=True) for a in acc], axis=0)
+
+    def col_pass(inverse):
+        wide = [
+            jnp.broadcast_to(inverse[p : p + 1, :], (SUBLANES, point_rows)) for p in range(shards)
+        ]
+
+        def step(g, carry):
+            rows = pl.ds(pl.multiple_of(g * SUBLANES, SUBLANES), SUBLANES)
+            total = kern[0, rows, :] * wide[0]
+            for p in range(1, shards):
+                total = total + kern[p, rows, :] * wide[p]
+            narrow = total[:, :LANES]
+            for t in range(1, tiles):
+                narrow = narrow + total[:, t * LANES : (t + 1) * LANES]
+            mass_cols[rows, :] = narrow
+            return carry
+
+        lax.fori_loop(0, groups, step, 0, unroll=2)
+        parts = [
+            jnp.sum(mass_cols[pl.ds(t * LANES, LANES), :].T, axis=0, keepdims=True)
+            for t in range(dual_rows)
+        ]
+        return jnp.concatenate(parts * (SUBLANES // dual_rows), axis=0)
+
+    def row_exchange(turn, part):
+        row_parts[turn, 0] = part
+        copies = []
+        for d in (6, 7, 2, 4, 3, 5, 1):
+            copy = pltpu.make_async_remote_copy(
+                src_ref=row_parts.at[turn, 0],
+                dst_ref=row_parts.at[turn, d],
+                send_sem=row_send.at[turn, d],
+                recv_sem=row_recv.at[turn, d],
+                device_id=(peer[d], z),
+                device_id_type=MESH,
+            )
+            copy.start()
+            copies.append(copy)
+        for copy in copies:
+            copy.wait()
+        rows = []
+        for p in range(shards):
+            total = part[p : p + 1, :]
+            for d in range(1, shards):
+                total = total + row_parts[turn, d, pl.ds(p ^ d, 1), :]
+            rows.append(total)
+        return jnp.concatenate(rows, axis=0)
+
+    def col_exchange(turn, part):
+        col_parts[turn, z] = part
+        copies = []
+        for k in range(1, replicas):
+            copy = pltpu.make_async_remote_copy(
+                src_ref=col_parts.at[turn, z],
+                dst_ref=col_parts.at[turn, z],
+                send_sem=col_send.at[turn, k],
+                recv_sem=col_recv.at[turn, k],
+                device_id=(me, zpeer[k]),
+                device_id_type=MESH,
+            )
+            copy.start()
+            copies.append(copy)
+        for copy in copies:
+            copy.wait()
+        total = col_parts[turn, 0]
+        for k in range(1, replicas):
+            total = total + col_parts[turn, k]
+        return total
+
+    row_turn = 0
+    col_turn = 0
+    for loop_counter in range(ITERS):
+        last = loop_counter == ITERS - 1
+        if loop_counter > 0:
+
+            def remake(slot, carry):
+                block_kernel(slot)
+                return carry
+
+            lax.fori_loop(0, shards, remake, 0)
+        for turn_index in range(SINK + 1):
+            scaling = jnp.exp(duals_now)
+            spread_scale(scaling)
+            inverse = 1.0 / row_exchange(row_turn, row_pass())
+            row_turn += 1
+            if turn_index < SINK:
+                mass = col_exchange(col_turn, col_pass(inverse) * scaling)
+                col_turn += 1
+                duals_now = duals_now + jnp.log(2.0 * target) - jnp.log(mass + target)
+
+        row_parts[row_turn - 1, 0] = inverse
+
+        def accumulate(slot, carry):
+            inv = row_parts[row_turn - 1, 0, pl.ds(slot, 1), :]
+            wide = jnp.concatenate([scale_cols[...]] * tiles, axis=1)
+            weights = (inv * kern[slot] * wide).astype(jnp.bfloat16)
+            product = jnp.dot(weights, units[slot], preferred_element_type=jnp.float32)
+
+            @pl.when(slot == 0)
+            def _():
+                sums[...] = product
+
+            @pl.when(slot > 0)
+            def _():
+                sums[...] += product
+
+            return carry
+
+        lax.fori_loop(0, shards, accumulate, 0)
+        copies = []
+        for k in range(1, replicas):
+            rows = pl.ds(pl.multiple_of(zpeer[k] * share, share), share)
+            sums_out[loop_counter, k] = sums[rows, :].astype(jnp.bfloat16)
+            copy = pltpu.make_async_remote_copy(
+                src_ref=sums_out.at[loop_counter, k],
+                dst_ref=sums_in.at[loop_counter, k],
+                send_sem=sum_send.at[loop_counter, k],
+                recv_sem=sum_recv.at[loop_counter, k],
+                device_id=(me, zpeer[k]),
+                device_id_type=MESH,
+            )
+            copy.start()
+            copies.append(copy)
+        for copy in copies:
+            copy.wait()
+        mine = pl.ds(pl.multiple_of(z * share, share), share)
+        total = sums[mine, :]
+        for k in range(1, replicas):
+            total = total + sums_in[loop_counter, k].astype(jnp.float32)
+        fresh = normalize(total)
+        if last:
+            dest = out_ref
+        else:
+            dest = cunit
+            fresh = normalize(fresh)
+        dest[mine, :] = fresh
+        copies = []
+        for k in range(1, replicas):
+            copy = pltpu.make_async_remote_copy(
+                src_ref=dest.at[mine],
+                dst_ref=dest.at[mine],
+                send_sem=new_send.at[loop_counter, k],
+                recv_sem=new_recv.at[loop_counter, k],
+                device_id=(me, zpeer[k]),
+                device_id_type=MESH,
+            )
+            copy.start()
+            copies.append(copy)
+        for copy in copies:
+            copy.wait()
+    duals_out_ref[...] = duals_now
+
+
+def fused_body(points, centroids, owners, blocks, duals):
+    point_rows, features = points.shape
+    shard_rows = centroids.shape[0]
+    shards = lax.axis_size("cent")
+    replicas = lax.axis_size("rep")
+    dims = (shards, replicas, point_rows, shard_rows, features)
+    dual_rows = shard_rows // LANES
+    share = shard_rows // replicas
+    wanted = owners.T[None, None, :, None, :] == jnp.arange(shards, dtype=jnp.int32).reshape(
+        -1, 1, 1, 1, 1
+    )
+    named = jnp.transpose(blocks, (1, 2, 0))[None, None] == jnp.arange(
+        BLOCKS_DEV, dtype=jnp.int32
+    ).reshape(1, -1, 1, 1, 1)
+    mask = jnp.any(jnp.logical_and(wanted, named), axis=(2, 3)).astype(jnp.float32)
+    dual_tile = jnp.concatenate([duals.reshape(dual_rows, LANES)] * (SUBLANES // dual_rows), axis=0)
+    vmem = pl.BlockSpec(memory_space=pltpu.VMEM)
+    row_turns = ITERS * (SINK + 1)
+    col_turns = ITERS * SINK
+    dma = pltpu.SemaphoreType.DMA
+    new_centroids, duals_out = pl.pallas_call(
+        functools.partial(fused_kernel, dims),
+        out_shape=(
+            jax.ShapeDtypeStruct((shard_rows, features), jnp.bfloat16),
+            jax.ShapeDtypeStruct((SUBLANES, LANES), jnp.float32),
+        ),
+        in_specs=[vmem] * 4,
+        out_specs=(vmem, vmem),
+        scratch_shapes=[
+            pltpu.VMEM((shards, point_rows, features), jnp.bfloat16),
+            pltpu.VMEM((shards, BLOCKS_DEV, point_rows), jnp.float32),
+            pltpu.VMEM((shards, shard_rows, point_rows), jnp.float32),
+            pltpu.VMEM((shard_rows, features), jnp.bfloat16),
+            pltpu.VMEM((shard_rows, LANES), jnp.float32),
+            pltpu.VMEM((shard_rows, LANES), jnp.float32),
+            pltpu.VMEM((shard_rows, features), jnp.float32),
+            pltpu.VMEM((row_turns, shards, shards, point_rows), jnp.float32),
+            pltpu.VMEM((col_turns, replicas, SUBLANES, LANES), jnp.float32),
+            pltpu.VMEM((ITERS, replicas, share, features), jnp.bfloat16),
+            pltpu.VMEM((ITERS, replicas, share, features), jnp.bfloat16),
+            dma((shards, 4, 3)),
+            dma((shards, 4)),
+            dma((shards,)),
+            dma((shards,)),
+            dma((row_turns, shards)),
+            dma((row_turns, shards)),
+            dma((col_turns, replicas)),
+            dma((col_turns, replicas)),
+            dma((ITERS, replicas)),
+            dma((ITERS, replicas)),
+            dma((ITERS, replicas)),
+            dma((ITERS, replicas)),
+        ],
+        compiler_params=pltpu.CompilerParams(
+            collective_id=0, has_side_effects=True, vmem_limit_bytes=VMEM_LIMIT
+        ),
+        name="fused_kmeans",
+    )(points, centroids, mask, dual_tile)
+    return new_centroids, duals_out[:dual_rows].reshape(shard_rows)
+
+
 def solution(mesh):
+    shards = mesh.shape["cent"]
+
+    def body(points, centroids, owners, blocks, duals):
+        point_rows, features = points.shape
+        shard_rows = centroids.shape[0]
+        plane_bytes = shards * point_rows * (2 * features + 4 * shard_rows)
+        cube = shards == 2**3 and shard_rows % LANES == 0 and SUBLANES % (shard_rows // LANES) == 0
+        if cube and plane_bytes <= VMEM_LIMIT // 3:
+            return fused_body(points, centroids, owners, blocks, duals)
+        return routed_body(points, centroids, owners, blocks, duals)
+
     return jax.shard_map(
         body,
         mesh=mesh,

time: 711 us -> 235 us (0.33)
  Pallas kernels: 0 us -> 224 us
  waiting for transfers between devices: 186 us -> 0 us
  local copies, waits for them, and re-layouts: 186 us -> 3.52 us
  blocking collectives: 175 us -> 0 us
  matrix products: 114 us -> 0 us
  between operations: 14.9 us -> 0.67 us
  other arithmetic: 14.6 us -> 2.84 us
  starting transfers between devices: 10.2 us -> 0 us
    pallas_call x0 -> x1, Pallas kernels: none -> 224 us  [fused_body(): pl.pallas_call(functools.partial(fused_kernel, dims), out_shape=(jax.Shap...]
    all_to_all x16 -> x0, blocking collectives: 115 us -> none  [the longest x8 58.3 us: body(): lax.all_to_all(partial_rows, 'cent', split_axis=0, concat_axis=0, tiled=T...]
    dot_general x18 -> x0, matrix products: 114 us -> none  [the longest x8 50.7 us: body(): jnp.dot(kernel, scaling, precision=lax.Precision.HIGHEST)]
    gather x16 -> x0, local copies, waits for them, and re-layouts: 109 us -> none  [the longest x8 54.9 us: body(): inverse[flat_point]]
    reduce_scatter x2 -> x0, waiting for transfers between devices: 80.1 us -> none  [body(): lax.psum_scatter(lax.dot_general(weights, slot_rows, (((0,), (0,)), ((),...]
    unnamed x31 -> x3, local copies, waits for them, and re-layouts: 63.3 us -> 2.27 us
    psum x6 -> x0, blocking collectives: 60 us -> none  [body(): column_mass = lax.psum(local_mass, 'rep')]
    all_gather x2 -> x0, waiting for transfers between devices: 54.7 us -> none  [body(): current = lax.all_gather(normalize(share_sums), 'rep', axis=0, tiled=True)]
  transfers between devices with their start and end apart: 6 -> 0, of which waited for: 5 -> 0; matrix products, arithmetic and copies ran while one was open for 4% -> 0% of each run, Pallas kernels for 0% -> 0%
where the time goes in v1:
time: 235 us; the launch traced here: 232 us
  Pallas kernels  224 us (95%)
  local copies, waits for them, and re-layouts  3.52 us (1%)
  other arithmetic  2.84 us (1%)
    pallas_call x1, Pallas kernels, fused_body(): pl.pallas_call(functools.partial(fused_kernel, dims), out_shape=(jax.Shap...  224 us

profile of v1, /device:TPU:0, one launch (start us, length us, event | category | flops | bytes accessed | tf_op | source)
XLA Modules:
  0.0 231.5 jit_solution(16225385470816247202)
XLA Ops:
  0.6 0.0 copy-start
  0.6 1.4 pad_maximum_fusion.duals_ref
  2.0 0.7 iota_compare_fusion.1
  2.7 0.0 copy-done
  2.7 0.1 and_reduce_fusion
  2.8 0.7 convert_element_type.3.mask_ref
  3.5 224.5 %fused_kmeans.1 = (bf16[512,1024]{1,0:T(8,128)(2,1)}, f32[8,128]{1,0:T(8,128)}) custom-call(bf16[512,1024]{1,0:T(8,128)(2,1)} %points_ref.1, bf16[512,1024]{1,0:T(8,128)(2,1)} %centroids_ref.1, f32[8,8,512]{2,1,0:T(8,128)} %convert_element_type.3.mask_ref, f32[8,128]{1,0:T(8,128)} %pad_maximum_fusion.duals_ref), custom_call_target="tpu_custom_call" | custom-call | tf_op jit(solution)/shard_map/fused_kmeans/pallas_call | solution.py:471
  228.0 1.3 slice_bitcast_fusion
  229.2 2.3 copy.8
  (1 shorter events, 0.0 us)
Async XLA Ops:
  0.6 2.1 copy-start

commit v2 on v1

--- a/solution.py
+++ b/solution.py
@@ -13,6 +13,7 @@
 ITERS = 2
 LANES = 128
 SUBLANES = 8
+OUT_PIECES = 4
 MESH = pl.DeviceIdType.MESH
 VMEM_LIMIT = 64000000
 
@@ -151,7 +152,9 @@
     pieces = 4
     piece = point_rows // pieces
     dual_rows = shard_rows // LANES
-    share = shard_rows // replicas
+    groups_out = OUT_PIECES
+    group = shard_rows // groups_out
+    cut = group // replicas
     target = point_rows * replicas / shard_rows
     inverse_soft = 1.0 / (features * softness_factor)
 
@@ -235,17 +238,20 @@
 
     cunit[...] = normalize(centroids_ref[...])
 
-    def block_kernel(slot):
+    def block_kernel(slot, start=0, count=shard_rows):
         scores = lax.dot_general(
-            cunit[...],
+            cunit[pl.ds(start, count), :],
             units[slot],
             (((1,), (1,)), ((), ())),
             preferred_element_type=jnp.float32,
         )
         marks = masks[slot]
-        for b in range(BLOCKS_DEV):
-            rows = slice(b * span, (b + 1) * span)
-            kern[slot, rows, :] = jnp.exp(scores[rows] * inverse_soft) * marks[b : b + 1, :]
+        for b in range(count // span):
+            rows = pl.ds(start + b * span, span)
+            mark = marks[start // span + b : start // span + b + 1, :]
+            kern[slot, rows, :] = (
+                jnp.exp(scores[b * span : (b + 1) * span] * inverse_soft) * mark
+            )
 
     block_kernel(0)
     for step in range(pieces):
@@ -368,13 +374,6 @@
     col_turn = 0
     for loop_counter in range(ITERS):
         last = loop_counter == ITERS - 1
-        if loop_counter > 0:
-
-            def remake(slot, carry):
-                block_kernel(slot)
-                return carry
-
-            lax.fori_loop(0, shards, remake, 0)
         for turn_index in range(SINK + 1):
             scaling = jnp.exp(duals_now)
             spread_scale(scaling)
@@ -387,64 +386,169 @@
 
         row_parts[row_turn - 1, 0] = inverse
 
-        def accumulate(slot, carry):
-            inv = row_parts[row_turn - 1, 0, pl.ds(slot, 1), :]
-            wide = jnp.concatenate([scale_cols[...]] * tiles, axis=1)
-            weights = (inv * kern[slot] * wide).astype(jnp.bfloat16)
-            product = jnp.dot(weights, units[slot], preferred_element_type=jnp.float32)
-
-            @pl.when(slot == 0)
+        dest = out_ref if last else cunit
+
+        def part_rows(i, q):
+            start = i * group + q * cut
+            if not isinstance(q, int):
+                start = pl.multiple_of(start, cut)
+            return pl.ds(start, cut)
+
+        def hop(way, src, dst, send_sem, recv_sem):
+            return pltpu.make_async_remote_copy(
+                src_ref=src,
+                dst_ref=dst,
+                send_sem=send_sem,
+                recv_sem=recv_sem,
+                device_id=(me, zpeer[1] if way == 0 else zpeer[replicas - 1]),
+                device_id_type=MESH,
+            )
+
+        def sum_hop(way, i, q):
+            return hop(
+                way,
+                sums_out.at[loop_counter, way, i, q],
+                sums_in.at[loop_counter, way, i, q],
+                sum_send.at[loop_counter, way, i, q],
+                sum_recv.at[loop_counter, way, i, q],
+            )
+
+        def new_hop(way, i, q):
+            return hop(
+                way,
+                dest.at[part_rows(i, q)],
+                dest.at[part_rows(i, q)],
+                new_send.at[loop_counter, way, i, q],
+                new_recv.at[loop_counter, way, i, q],
+            )
+
+        def accumulate(i):
+            rows = pl.ds(i * group, group)
+            wide = jnp.concatenate([scale_cols[rows, :]] * tiles, axis=1)
+
+            def step(slot, acc):
+                inv = row_parts[row_turn - 1, 0, pl.ds(slot, 1), :]
+                weights = (inv * kern[slot, rows, :] * wide).astype(jnp.bfloat16)
+                return acc + jnp.dot(weights, units[slot], preferred_element_type=jnp.float32)
+
+            zero = jnp.zeros((group, features), jnp.float32)
+            sums[rows, :] = lax.fori_loop(0, shards, step, zero)
+
+            def first(way, q):
+                sums_out[loop_counter, way, i, q] = sums[part_rows(i, q), :].astype(jnp.bfloat16)
+                sum_hop(way, i, q).start()
+
+            @pl.when(z == 0)
             def _():
-                sums[...] = product
-
-            @pl.when(slot > 0)
+                for q in range(replicas - 1, 0, -1):
+                    first(0, q)
+
+            @pl.when(z == replicas - 1)
             def _():
-                sums[...] += product
-
-            return carry
-
-        lax.fori_loop(0, shards, accumulate, 0)
-        copies = []
-        for k in range(1, replicas):
-            rows = pl.ds(pl.multiple_of(zpeer[k] * share, share), share)
-            sums_out[loop_counter, k] = sums[rows, :].astype(jnp.bfloat16)
-            copy = pltpu.make_async_remote_copy(
-                src_ref=sums_out.at[loop_counter, k],
-                dst_ref=sums_in.at[loop_counter, k],
-                send_sem=sum_send.at[loop_counter, k],
-                recv_sem=sum_recv.at[loop_counter, k],
-                device_id=(me, zpeer[k]),
-                device_id_type=MESH,
-            )
-            copy.start()
-            copies.append(copy)
-        for copy in copies:
-            copy.wait()
-        mine = pl.ds(pl.multiple_of(z * share, share), share)
-        total = sums[mine, :]
-        for k in range(1, replicas):
-            total = total + sums_in[loop_counter, k].astype(jnp.float32)
-        fresh = normalize(total)
-        if last:
-            dest = out_ref
-        else:
-            dest = cunit
-            fresh = normalize(fresh)
-        dest[mine, :] = fresh
-        copies = []
-        for k in range(1, replicas):
-            copy = pltpu.make_async_remote_copy(
-                src_ref=dest.at[mine],
-                dst_ref=dest.at[mine],
-                send_sem=new_send.at[loop_counter, k],
-                recv_sem=new_recv.at[loop_counter, k],
-                device_id=(me, zpeer[k]),
-                device_id_type=MESH,
-            )
-            copy.start()
-            copies.append(copy)
-        for copy in copies:
-            copy.wait()
+                for q in range(replicas - 1):
+                    first(1, q)
+
+        def relay_sums(i):
+            def onward(way, q):
+                sum_hop(way, i, q).wait_recv()
+                total = sums[part_rows(i, q), :] + sums_in[loop_counter, way, i, q].astype(
+                    jnp.float32
+                )
+                sums_out[loop_counter, way, i, q] = total.astype(jnp.bfloat16)
+                sum_hop(way, i, q).start()
+
+            for q in range(replicas - 1, 0, -1):
+                mirror = replicas - 1 - q
+
+                @pl.when(jnp.logical_and(z > 0, z < q))
+                def _():
+                    onward(0, q)
+
+                @pl.when(jnp.logical_and(z < replicas - 1, z > mirror))
+                def _():
+                    onward(1, mirror)
+
+        def finish_sums(i):
+            mine = part_rows(i, z)
+
+            @pl.when(z > 0)
+            def _():
+                sum_hop(0, i, z).wait_recv()
+                sums[mine, :] += sums_in[loop_counter, 0, i, z].astype(jnp.float32)
+
+            @pl.when(z < replicas - 1)
+            def _():
+                sum_hop(1, i, z).wait_recv()
+                sums[mine, :] += sums_in[loop_counter, 1, i, z].astype(jnp.float32)
+
+            fresh = normalize(sums[mine, :])
+            dest[mine, :] = fresh if last else normalize(fresh)
+
+            @pl.when(z < replicas - 1)
+            def _():
+                new_hop(0, i, z).start()
+
+            @pl.when(z > 0)
+            def _():
+                new_hop(1, i, z).start()
+
+        def relay_new(i):
+            for q in range(replicas - 1):
+                near = replicas - 2 - q
+                mirror = replicas - 1 - near
+
+                @pl.when(z > near)
+                def _():
+                    new_hop(0, i, near).wait_recv()
+
+                @pl.when(jnp.logical_and(z > near, z < replicas - 1))
+                def _():
+                    new_hop(0, i, near).start()
+
+                @pl.when(z < mirror)
+                def _():
+                    new_hop(1, i, mirror).wait_recv()
+
+                @pl.when(jnp.logical_and(z < mirror, z > 0))
+                def _():
+                    new_hop(1, i, mirror).start()
+
+        def remake(i):
+            if last:
+                return
+
+            def step(slot, carry):
+                block_kernel(slot, i * group, group)
+                return carry
+
+            lax.fori_loop(0, shards, step, 0)
+
+        for i in range(groups_out):
+            accumulate(i)
+        stages = (relay_sums, finish_sums, relay_new, remake)
+        for step in range(groups_out + len(stages) - 1):
+            for lag, stage in enumerate(stages):
+                if 0 <= step - lag < groups_out:
+                    stage(step - lag)
+        for i in range(groups_out):
+            for q in range(replicas):
+
+                @pl.when(z < q)
+                def _():
+                    sum_hop(0, i, q).wait_send()
+
+                @pl.when(z > q)
+                def _():
+                    sum_hop(1, i, q).wait_send()
+
+                @pl.when(jnp.logical_and(z >= q, z < replicas - 1))
+                def _():
+                    new_hop(0, i, q).wait_send()
+
+                @pl.when(jnp.logical_and(z <= q, z > 0))
+                def _():
+                    new_hop(1, i, q).wait_send()
+
     duals_out_ref[...] = duals_now
 
 
@@ -455,7 +559,7 @@
     replicas = lax.axis_size("rep")
     dims = (shards, replicas, point_rows, shard_rows, features)
     dual_rows = shard_rows // LANES
-    share = shard_rows // replicas
+    cut = shard_rows // (OUT_PIECES * replicas)
     wanted = owners.T[None, None, :, None, :] == jnp.arange(shards, dtype=jnp.int32).reshape(
         -1, 1, 1, 1, 1
     )
@@ -486,8 +590,8 @@
             pltpu.VMEM((shard_rows, features), jnp.float32),
             pltpu.VMEM((row_turns, shards, shards, point_rows), jnp.float32),
             pltpu.VMEM((col_turns, replicas, SUBLANES, LANES), jnp.float32),
-            pltpu.VMEM((ITERS, replicas, share, features), jnp.bfloat16),
-            pltpu.VMEM((ITERS, replicas, share, features), jnp.bfloat16),
+            pltpu.VMEM((ITERS, 2, OUT_PIECES, replicas, cut, features), jnp.bfloat16),
+            pltpu.VMEM((ITERS, 2, OUT_PIECES, replicas, cut, features), jnp.bfloat16),
             dma((shards, 4, 3)),
             dma((shards, 4)),
             dma((shards,)),
@@ -496,10 +600,10 @@
             dma((row_turns, shards)),
             dma((col_turns, replicas)),
             dma((col_turns, replicas)),
-            dma((ITERS, replicas)),
-            dma((ITERS, replicas)),
-            dma((ITERS, replicas)),
-            dma((ITERS, replicas)),
+            dma((ITERS, 2, OUT_PIECES, replicas)),
+            dma((ITERS, 2, OUT_PIECES, replicas)),
+            dma((ITERS, 2, OUT_PIECES, replicas)),
+            dma((ITERS, 2, OUT_PIECES, replicas)),
         ],
         compiler_params=pltpu.CompilerParams(
             collective_id=0, has_side_effects=True, vmem_limit_bytes=VMEM_LIMIT

time: 235 us -> 289 us (1.23); the launches traced: 232 us -> 289 us
  Pallas kernels: 224 us -> 282 us
    pallas_call x1, Pallas kernels: 224 us -> 282 us  [fused_body(): pl.pallas_call(functools.partial(fused_kernel, dims), out_shape=(jax.Shap...]
where the time goes in v2:
time: 289 us
  Pallas kernels  282 us (98%)
  local copies, waits for them, and re-layouts  3.52 us (1%)
    pallas_call x1, Pallas kernels, fused_body(): pl.pallas_call(functools.partial(fused_kernel, dims), out_shape=(jax.Shap...  282 us

profile of v2, /device:TPU:0, one launch (start us, length us, event | category | flops | bytes accessed | tf_op | source)
XLA Modules:
  0.0 288.6 jit_solution(10320342590626500942)
XLA Ops:
  0.6 0.0 copy-start
  0.6 1.4 pad_maximum_fusion.duals_ref
  2.0 0.7 iota_compare_fusion.1
  2.7 0.0 copy-done
  2.7 0.1 and_reduce_fusion
  2.8 0.7 convert_element_type.3.mask_ref
  3.5 281.6 %fused_kmeans.1 = (bf16[512,1024]{1,0:T(8,128)(2,1)}, f32[8,128]{1,0:T(8,128)}) custom-call(bf16[512,1024]{1,0:T(8,128)(2,1)} %points_ref.1, bf16[512,1024]{1,0:T(8,128)(2,1)} %centroids_ref.1, f32[8,8,512]{2,1,0:T(8,128)} %convert_element_type.3.mask_ref, f32[8,128]{1,0:T(8,128)} %pad_maximum_fusion.duals_ref), custom_call_target="tpu_custom_call" | custom-call | tf_op jit(solution)/shard_map/fused_kmeans/pallas_call | solution.py:575
  285.1 1.3 slice_bitcast_fusion
  286.3 2.3 copy.8
  (1 shorter events, 0.0 us)
Async XLA Ops:
  0.6 2.1 copy-start

commit v3 on v2

--- a/solution.py
+++ b/solution.py
@@ -174,6 +174,13 @@
     peer = [rel(d) for d in range(shards)]
     zpeer = [(z + k) % replicas for k in range(replicas)]
 
+    at_end = jnp.logical_or(z == 0, z == replicas - 1)
+    in_mid = jnp.logical_not(at_end)
+    partner = z + 1 - 2 * (z % 2)
+    low = z // 2
+    far_end = 3 - 3 * low
+    far_mid = 2 - low
+
     barrier = pltpu.get_barrier_semaphore()
     for d in range(1, shards):
         pl.semaphore_signal(barrier, inc=1, device_id=(peer[d], z), device_id_type=MESH)
@@ -394,33 +401,34 @@
                 start = pl.multiple_of(start, cut)
             return pl.ds(start, cut)
 
-        def hop(way, src, dst, send_sem, recv_sem):
+        def sum_copy(i, source, landing, to):
             return pltpu.make_async_remote_copy(
-                src_ref=src,
-                dst_ref=dst,
-                send_sem=send_sem,
-                recv_sem=recv_sem,
-                device_id=(me, zpeer[1] if way == 0 else zpeer[replicas - 1]),
+                src_ref=sums_out.at[loop_counter, i, source],
+                dst_ref=sums_in.at[loop_counter, i, landing],
+                send_sem=sum_send.at[loop_counter, i, source],
+                recv_sem=sum_recv.at[loop_counter, i, landing],
+                device_id=(me, to),
                 device_id_type=MESH,
             )
 
-        def sum_hop(way, i, q):
-            return hop(
-                way,
-                sums_out.at[loop_counter, way, i, q],
-                sums_in.at[loop_counter, way, i, q],
-                sum_send.at[loop_counter, way, i, q],
-                sum_recv.at[loop_counter, way, i, q],
+        def sum_arrive(i, landing):
+            ref = sums_in.at[loop_counter, i, landing]
+            pltpu.make_async_copy(ref, ref, sum_recv.at[loop_counter, i, landing]).wait()
+            return sums_in[loop_counter, i, landing].astype(jnp.float32)
+
+        def new_copy(i, q, to, number):
+            return pltpu.make_async_remote_copy(
+                src_ref=dest.at[part_rows(i, q)],
+                dst_ref=dest.at[part_rows(i, q)],
+                send_sem=new_send.at[loop_counter, i, number],
+                recv_sem=new_recv.at[loop_counter, i, q],
+                device_id=(me, to),
+                device_id_type=MESH,
             )
 
-        def new_hop(way, i, q):
-            return hop(
-                way,
-                dest.at[part_rows(i, q)],
-                dest.at[part_rows(i, q)],
-                new_send.at[loop_counter, way, i, q],
-                new_recv.at[loop_counter, way, i, q],
-            )
+        def new_arrive(i, q):
+            ref = dest.at[part_rows(i, q)]
+            pltpu.make_async_copy(ref, ref, new_recv.at[loop_counter, i, q]).wait()
 
         def accumulate(i):
             rows = pl.ds(i * group, group)
@@ -434,84 +442,47 @@
             zero = jnp.zeros((group, features), jnp.float32)
             sums[rows, :] = lax.fori_loop(0, shards, step, zero)
 
-            def first(way, q):
-                sums_out[loop_counter, way, i, q] = sums[part_rows(i, q), :].astype(jnp.bfloat16)
-                sum_hop(way, i, q).start()
-
-            @pl.when(z == 0)
+            def raw(source, q):
+                sums_out[loop_counter, i, source] = sums[part_rows(i, q), :].astype(jnp.bfloat16)
+                sum_copy(i, source, source, partner).start()
+
+            @pl.when(at_end)
             def _():
-                for q in range(replicas - 1, 0, -1):
-                    first(0, q)
-
-            @pl.when(z == replicas - 1)
+                raw(2, far_end)
+                raw(3, far_mid)
+
+            raw(0, partner)
+
+        def pair_sums(i):
+            @pl.when(in_mid)
             def _():
-                for q in range(replicas - 1):
-                    first(1, q)
-
-        def relay_sums(i):
-            def onward(way, q):
-                sum_hop(way, i, q).wait_recv()
-                total = sums[part_rows(i, q), :] + sums_in[loop_counter, way, i, q].astype(
-                    jnp.float32
-                )
-                sums_out[loop_counter, way, i, q] = total.astype(jnp.bfloat16)
-                sum_hop(way, i, q).start()
-
-            for q in range(replicas - 1, 0, -1):
-                mirror = replicas - 1 - q
-
-                @pl.when(jnp.logical_and(z > 0, z < q))
-                def _():
-                    onward(0, q)
-
-                @pl.when(jnp.logical_and(z < replicas - 1, z > mirror))
-                def _():
-                    onward(1, mirror)
+                for source, q in ((2, far_end), (3, far_mid)):
+                    total = sum_arrive(i, source) + sums[part_rows(i, q), :]
+                    sums_out[loop_counter, i, source] = total.astype(jnp.bfloat16)
+                    sum_copy(i, source, 1, q).start()
 
         def finish_sums(i):
             mine = part_rows(i, z)
-
-            @pl.when(z > 0)
+            total = sums[mine, :] + sum_arrive(i, 0)
+            fresh = normalize(total + sum_arrive(i, 1))
+            dest[mine, :] = fresh if last else normalize(fresh)
+            new_copy(i, z, far_mid, 1).start()
+            new_copy(i, z, partner, 0).start()
+
+        def forward_new(i):
+            @pl.when(in_mid)
             def _():
-                sum_hop(0, i, z).wait_recv()
-                sums[mine, :] += sums_in[loop_counter, 0, i, z].astype(jnp.float32)
-
-            @pl.when(z < replicas - 1)
+                for number, q in ((3, far_mid), (2, far_end)):
+                    new_arrive(i, q)
+                    new_copy(i, q, partner, number).start()
+
+            new_arrive(i, partner)
+
+        def end_new(i):
+            @pl.when(at_end)
             def _():
-                sum_hop(1, i, z).wait_recv()
-                sums[mine, :] += sums_in[loop_counter, 1, i, z].astype(jnp.float32)
-
-            fresh = normalize(sums[mine, :])
-            dest[mine, :] = fresh if last else normalize(fresh)
-
-            @pl.when(z < replicas - 1)
-            def _():
-                new_hop(0, i, z).start()
-
-            @pl.when(z > 0)
-            def _():
-                new_hop(1, i, z).start()
-
-        def relay_new(i):
-            for q in range(replicas - 1):
-                near = replicas - 2 - q
-                mirror = replicas - 1 - near
-
-                @pl.when(z > near)
-                def _():
-                    new_hop(0, i, near).wait_recv()
-
-                @pl.when(jnp.logical_and(z > near, z < replicas - 1))
-                def _():
-                    new_hop(0, i, near).start()
-
-                @pl.when(z < mirror)
-                def _():
-                    new_hop(1, i, mirror).wait_recv()
-
-                @pl.when(jnp.logical_and(z < mirror, z > 0))
-                def _():
-                    new_hop(1, i, mirror).start()
+                new_arrive(i, far_mid)
+                new_arrive(i, far_end)
 
         def remake(i):
             if last:
@@ -523,31 +494,22 @@
 
             lax.fori_loop(0, shards, step, 0)
 
-        for i in range(groups_out):
-            accumulate(i)
-        stages = (relay_sums, finish_sums, relay_new, remake)
-        for step in range(groups_out + len(stages) - 1):
-            for lag, stage in enumerate(stages):
+        stages = (accumulate, pair_sums, finish_sums, forward_new, end_new, remake)
+        lags = (0, 1, 2, 3, 4, 4)
+        for step in range(groups_out + lags[-1]):
+            for lag, stage in zip(lags, stages):
                 if 0 <= step - lag < groups_out:
                     stage(step - lag)
         for i in range(groups_out):
-            for q in range(replicas):
-
-                @pl.when(z < q)
-                def _():
-                    sum_hop(0, i, q).wait_send()
-
-                @pl.when(z > q)
-                def _():
-                    sum_hop(1, i, q).wait_send()
-
-                @pl.when(jnp.logical_and(z >= q, z < replicas - 1))
-                def _():
-                    new_hop(0, i, q).wait_send()
-
-                @pl.when(jnp.logical_and(z <= q, z > 0))
-                def _():
-                    new_hop(1, i, q).wait_send()
+            for source in (0, 2, 3):
+                sum_copy(i, source, source, partner).wait_send()
+            new_copy(i, z, partner, 0).wait_send()
+            new_copy(i, z, far_mid, 1).wait_send()
+
+            @pl.when(in_mid)
+            def _():
+                new_copy(i, far_end, partner, 2).wait_send()
+                new_copy(i, far_mid, partner, 3).wait_send()
 
     duals_out_ref[...] = duals_now
 
@@ -590,8 +552,8 @@
             pltpu.VMEM((shard_rows, features), jnp.float32),
             pltpu.VMEM((row_turns, shards, shards, point_rows), jnp.float32),
             pltpu.VMEM((col_turns, replicas, SUBLANES, LANES), jnp.float32),
-            pltpu.VMEM((ITERS, 2, OUT_PIECES, replicas, cut, features), jnp.bfloat16),
-            pltpu.VMEM((ITERS, 2, OUT_PIECES, replicas, cut, features), jnp.bfloat16),
+            pltpu.VMEM((ITERS, OUT_PIECES, 4, cut, features), jnp.bfloat16),
+            pltpu.VMEM((ITERS, OUT_PIECES, 4, cut, features), jnp.bfloat16),
             dma((shards, 4, 3)),
             dma((shards, 4)),
             dma((shards,)),
@@ -600,10 +562,10 @@
             dma((row_turns, shards)),
             dma((col_turns, replicas)),
             dma((col_turns, replicas)),
-            dma((ITERS, 2, OUT_PIECES, replicas)),
-            dma((ITERS, 2, OUT_PIECES, replicas)),
-            dma((ITERS, 2, OUT_PIECES, replicas)),
-            dma((ITERS, 2, OUT_PIECES, replicas)),
+            dma((ITERS, OUT_PIECES, 4)),
+            dma((ITERS, OUT_PIECES, 4)),
+            dma((ITERS, OUT_PIECES, 4)),
+            dma((ITERS, OUT_PIECES, 4)),
         ],
         compiler_params=pltpu.CompilerParams(
             collective_id=0, has_side_effects=True, vmem_limit_bytes=VMEM_LIMIT
@@ -620,7 +582,7 @@
         point_rows, features = points.shape
         shard_rows = centroids.shape[0]
         plane_bytes = shards * point_rows * (2 * features + 4 * shard_rows)
-        cube = shards == 2**3 and shard_rows % LANES == 0 and SUBLANES % (shard_rows // LANES) == 0
+        cube = shards == 2**3 and mesh.shape["rep"] == 2 * 2 and shard_rows % LANES == 0 and SUBLANES % (shard_rows // LANES) == 0
         if cube and plane_bytes <= VMEM_LIMIT // 3:
             return fused_body(points, centroids, owners, blocks, duals)
         return routed_body(points, centroids, owners, blocks, duals)

time: 289 us -> 206 us (0.71)
  Pallas kernels: 282 us -> 199 us
    pallas_call x1, Pallas kernels: 282 us -> 199 us  [fused_body(): pl.pallas_call(functools.partial(fused_kernel, dims), out_shape=(jax.Shap...]
where the time goes in v3:
time: 206 us
  Pallas kernels  199 us (97%)
  local copies, waits for them, and re-layouts  3.52 us (2%)
  other arithmetic  2.84 us (1%)
    pallas_call x1, Pallas kernels, fused_body(): pl.pallas_call(functools.partial(fused_kernel, dims), out_shape=(jax.Shap...  199 us

profile of v3, /device:TPU:0, one launch (start us, length us, event | category | flops | bytes accessed | tf_op | source)
XLA Modules:
  0.0 205.8 jit_solution(16132538669602470279)
XLA Ops:
  0.6 0.0 copy-start
  0.6 1.4 pad_maximum_fusion.duals_ref
  2.0 0.7 iota_compare_fusion.1
  2.7 0.0 copy-done
  2.7 0.1 and_reduce_fusion
  2.8 0.7 convert_element_type.3.mask_ref
  3.5 198.8 %fused_kmeans.1 = (bf16[512,1024]{1,0:T(8,128)(2,1)}, f32[8,128]{1,0:T(8,128)}) custom-call(bf16[512,1024]{1,0:T(8,128)(2,1)} %points_ref.1, bf16[512,1024]{1,0:T(8,128)(2,1)} %centroids_ref.1, f32[8,8,512]{2,1,0:T(8,128)} %convert_element_type.3.mask_ref, f32[8,128]{1,0:T(8,128)} %pad_maximum_fusion.duals_ref), custom_call_target="tpu_custom_call" | custom-call | tf_op jit(solution)/shard_map/fused_kmeans/pallas_call | solution.py:537
  202.3 1.3 slice_bitcast_fusion
  203.6 2.3 %copy.8 = bf16[512,1024]{1,0:T(8,128)(2,1)} copy(bf16[512,1024]{1,0:T(8,128)(2,1)} %get-tuple-element.8) | data formatting | bytes 2097152
  (1 shorter events, 0.0 us)
Async XLA Ops:
  0.6 2.1 %copy-start = (s32[512,2,4]{0,2,1:T(4,128)S(1)}, s32[512,2,4]{0,2,1:T(4,128)}, u32[]{:S(2)}) copy-start(s32[512,2,4]{0,2,1:T(4,128)} %param.8) | copy-start | bytes 49156

commit v4 on v3

--- a/solution.py
+++ b/solution.py
@@ -245,20 +245,25 @@
 
     cunit[...] = normalize(centroids_ref[...])
 
-    def block_kernel(slot, start=0, count=shard_rows):
+    def block_kernel(slot, start=0, count=shard_rows, first=0, width=point_rows):
+        held = pl.ds(first, width)
         scores = lax.dot_general(
             cunit[pl.ds(start, count), :],
-            units[slot],
+            units[slot, held, :],
             (((1,), (1,)), ((), ())),
             preferred_element_type=jnp.float32,
         )
-        marks = masks[slot]
+        marks = masks[slot, :, held]
         for b in range(count // span):
             rows = pl.ds(start + b * span, span)
             mark = marks[start // span + b : start // span + b + 1, :]
-            kern[slot, rows, :] = (
+            kern[slot, rows, held] = (
                 jnp.exp(scores[b * span : (b + 1) * span] * inverse_soft) * mark
             )
+
+    def half_kernels(halves):
+        for slot, chunks in halves:
+            block_kernel(slot, first=min(chunks) * piece, width=2 * piece)
 
     block_kernel(0)
     for step in range(pieces):
@@ -282,15 +287,24 @@
             push(6, order_x[step - 2], 1)
             arrive(6, order_y[step - 2])
             push(6, order_y[step - 2], 1)
-    for slot in (2, 4, 6, 3, 5, 7):
-        if slot % 2:
-            for chunk in range(pieces):
-                arrive(slot, chunk)
-        block_kernel(slot)
+        if step == 2:
+            for slot, chunks in ((3, order_x[:2]), (5, order_y[:2])):
+                for chunk in chunks:
+                    arrive(slot, chunk)
+            half_kernels(((2, order_x[:2]), (4, order_y[:2]), (3, order_x[:2]), (5, order_y[:2])))
+    half_kernels(((2, order_x[2:]), (4, order_y[2:])))
+    for slot, chunks in ((3, order_x[2:]), (5, order_y[2:])):
+        for chunk in chunks:
+            arrive(slot, chunk)
+        half_kernels(((slot, chunks),))
+    half_kernels(((6, order_x[:2]), (6, order_y[:2])))
+    for chunk in range(pieces):
+        arrive(7, chunk)
+    half_kernels(((7, order_x[:2]), (7, order_y[:2])))
     for copy in unit_copies.values():
         copy.wait_send()
 
-    duals_now = duals_ref[...]
+    duals_now = jnp.concatenate([duals_ref[...]] * (SUBLANES // dual_rows), axis=0)
     groups = shard_rows // SUBLANES
     tiles = point_rows // LANES
 
@@ -511,7 +525,7 @@
                 new_copy(i, far_end, partner, 2).wait_send()
                 new_copy(i, far_mid, partner, 3).wait_send()
 
-    duals_out_ref[...] = duals_now
+    duals_out_ref[...] = duals_now[:dual_rows]
 
 
 def fused_body(points, centroids, owners, blocks, duals):
@@ -529,7 +543,7 @@
         BLOCKS_DEV, dtype=jnp.int32
     ).reshape(1, -1, 1, 1, 1)
     mask = jnp.any(jnp.logical_and(wanted, named), axis=(2, 3)).astype(jnp.float32)
-    dual_tile = jnp.concatenate([duals.reshape(dual_rows, LANES)] * (SUBLANES // dual_rows), axis=0)
+    dual_tile = duals.reshape(dual_rows, LANES)
     vmem = pl.BlockSpec(memory_space=pltpu.VMEM)
     row_turns = ITERS * (SINK + 1)
     col_turns = ITERS * SINK
@@ -538,7 +552,7 @@
         functools.partial(fused_kernel, dims),
         out_shape=(
             jax.ShapeDtypeStruct((shard_rows, features), jnp.bfloat16),
-            jax.ShapeDtypeStruct((SUBLANES, LANES), jnp.float32),
+            jax.ShapeDtypeStruct((dual_rows, LANES), jnp.float32),
         ),
         in_specs=[vmem] * 4,
         out_specs=(vmem, vmem),
@@ -572,7 +586,7 @@
         ),
         name="fused_kmeans",
     )(points, centroids, mask, dual_tile)
-    return new_centroids, duals_out[:dual_rows].reshape(shard_rows)
+    return new_centroids, duals_out.reshape(shard_rows)
 
 
 def solution(mesh):

time: 206 us -> 203 us (0.985)
  no operation moved by 1% of the time
where the time goes in v4:
time: 203 us
  Pallas kernels  198 us (98%)
  local copies, waits for them, and re-layouts  2.85 us (1%)
    pallas_call x1, Pallas kernels, fused_body(): pl.pallas_call(functools.partial(fused_kernel, dims), out_shape=(jax.Shap...  198 us

profile of v4, /device:TPU:0, one launch (start us, length us, event | category | flops | bytes accessed | tf_op | source)
XLA Modules:
  0.0 203.2 jit_solution(13536036658658766616)
XLA Ops:
  0.6 0.0 copy-start
  0.6 0.7 iota_compare_fusion.1
  1.4 0.0 copy-done
  1.4 0.1 and_reduce_fusion
  1.5 0.7 convert_element_type.3.mask_ref
  2.2 198.2 %fused_kmeans.1 = (bf16[512,1024]{1,0:T(8,128)(2,1)}, f32[4,128]{1,0:T(4,128)}) custom-call(bf16[512,1024]{1,0:T(8,128)(2,1)} %points_ref.1, bf16[512,1024]{1,0:T(8,128)(2,1)} %centroids_ref.1, f32[8,8,512]{2,1,0:T(8,128)} %convert_element_type.3.mask_ref, f32[4,128]{1,0:T(4,128)} %bitcast.6), custom_call_target="tpu_custom_call" | custom-call | tf_op jit(solution)/shard_map/fused_kmeans/pallas_call | solution.py:551
  200.3 0.0 copy-start.1
  200.3 2.3 %copy.9 = bf16[512,1024]{1,0:T(8,128)(2,1)} copy(bf16[512,1024]{1,0:T(8,128)(2,1)} %get-tuple-element.8) | data formatting | bytes 2097152
  202.6 0.0 copy-done.1
  202.6 0.6 copy.10
  (1 shorter events, 0.0 us)
Async XLA Ops:
  0.6 0.7 copy-start
  200.3 2.3 %copy-start.1 = (f32[4,128]{1,0:T(4,128)S(1)}, f32[4,128]{1,0:T(4,128)}, u32[]{:S(2)}) copy-start(f32[4,128]{1,0:T(4,128)} %get-tuple-element.5) | copy-start | bytes 6148
